TPU v7x, 512 devices: a whole 4x8x8 slice. The times are simulated.
512 devices in a mesh: rows: 32 (over z, x), piv: 16 (over y, core).
Axes of the slice: x: 4, y: 8, z: 8, core: 2. Of those that a mesh axis runs over, the one named last changes fastest.
Arguments:
- ancestor_sol: float32 [1024, 32768], P('piv', 'rows'), may hold values from -6 to 6
- front_map: int32 [256], P('rows'), may hold values from 0 to 255, each once
- lower_panel: float32 [32768, 12288], P('rows', 'piv'), may hold values from -0.03125 to 0.03125
- inverse_factor: float32 [12288, 12288], P('piv', 'rows'), as said below
- right_side: float32 [1024, 12288], P(None, ('piv', 'rows')), may hold values from -6 to 6
- child_start: int32 [128], P('rows'), may hold values from 0 to 12287, as said below
- child_len: int32 [128], P('rows'), may hold values from 1 to 128, as said below
Outputs:
- child_blocks: float32 [1024, 16384], P('piv', 'rows')
Inputs may be any that keep to these rules, and one draw needn't show every extreme that they name: Child block c lies within pivots k * 384 to (k + 1) * 384 - 1, with k = c // 4; child_start[c] + child_len[c] <= (k + 1) * 384. `child_len`: child block 0 is full. inverse_factor is lower triangular with a diagonal in [0.5, 2].
All inputs are finite; a program needn't handle non-finite values.
Results may differ from a plain program's by a relative error of at most 0.000088.
Values sent between devices are 32-bit elements; how exact they have to be, the bound alone decides.
No kernel may reach another device: no remote copies, remote signals or barrier semaphores. Data moves between devices by JAX's collectives and lax.ppermute only.
A program may use at most 64 MiB of HBM per device.

v0:
```python
import jax
import jax.numpy as jnp
from jax import lax
from jax.sharding import Mesh
from jax.sharding import PartitionSpec as P

ROW_BLK = 128
CHILD_BLK = 128
ROWS = ("rows_0", "rows_1")
PIV_ROWS = ("piv", "rows_0", "rows_1")


def scatter_axes(value, axes, dim):
    if not axes:
        return value
    nearer = lax.psum_scatter(value, axes[0], scatter_dimension=dim, tiled=True)
    return scatter_axes(nearer, axes[1:], dim)


def gather_axes(value, axes, dim):
    for axis in reversed(axes):
        value = lax.all_gather(value, axis, axis=dim, tiled=True)
    return value


def in_blocks(value, dim, size):
    lengths = value.shape
    parts = value.reshape(*lengths[:dim], size, lengths[dim] // size, *lengths[dim + 1 :])
    return jnp.moveaxis(parts, dim, 0)


def sent_and_summed(value, axis, dim):
    parts = in_blocks(value, dim, lax.axis_size(axis))
    arrived = lax.all_to_all(parts, axis, split_axis=0, concat_axis=0, tiled=True)
    return arrived.sum(axis=0)


def body(ancestor_sol, front_map, lower_panel, inverse_factor, right_side, child_start, child_len):
    local_srcs = ancestor_sol.shape[0]
    count = front_map.shape[0]
    empty = jnp.zeros((local_srcs, count * ROW_BLK), jnp.float32)
    carry = empty
    piece = lax.all_gather(ancestor_sol, ROWS, axis=1, tiled=True)
    width = piece.shape[1]
    for block in range(count):
        offset = front_map[block] * ROW_BLK
        inside = (offset >= 0) & (offset < width)
        taken = lax.dynamic_slice_in_dim(piece, jnp.clip(offset, 0, width - ROW_BLK), ROW_BLK, 1)
        previous = carry[:, block * ROW_BLK : (block + 1) * ROW_BLK]
        carry = carry.at[:, block * ROW_BLK : (block + 1) * ROW_BLK].set(
            jnp.where(inside, taken, previous)
        )
    boundary = lax.all_gather(carry, "piv", axis=0, tiled=True)
    coupled = jnp.dot(
        boundary, lower_panel, precision=lax.Precision.HIGHEST, preferred_element_type=jnp.float32
    )
    span = inverse_factor.shape[1]
    share = right_side - scatter_axes(coupled, ROWS, 1)
    partial_sol = jnp.dot(
        gather_axes(share, ROWS, 1),
        inverse_factor,
        precision=lax.Precision.HIGHEST,
        preferred_element_type=jnp.float32,
    )
    slots = jnp.arange(CHILD_BLK, dtype=jnp.int32)
    local_first = child_start - lax.axis_index(ROWS) * span
    columns = jnp.clip(local_first[:, None] + slots[None, :], 0, span - 1).reshape(-1)
    valid = (slots[None, :] < child_len[:, None]).reshape(-1)[None, :]
    summed = sent_and_summed(partial_sol, "piv", 0)
    picked = jnp.take(summed, columns, axis=1)
    return jnp.where(valid, picked, jnp.zeros_like(picked))


def solution(mesh):
    torus = Mesh(mesh.devices.reshape(8, 4, mesh.shape["piv"]), ("rows_0", "rows_1", "piv"))
    return jax.shard_map(
        body,
        mesh=torus,
        in_specs=(
            P("piv", ROWS),
            P(ROWS),
            P(ROWS, "piv"),
            P("piv", ROWS),
            P(None, PIV_ROWS),
            P(ROWS),
            P(ROWS),
        ),
        out_specs=P("piv", ROWS),
        check_vma=False,
    )
```

profile of v0, /device:TPU:1, one launch (start us, length us, event | category | flops | bytes accessed | tf_op | source)
XLA Modules:
  0.0 392.0 jit_solution(8113103257739380664)
XLA Ops:
  6.5 0.7 all-gather.4.cloned.1.call-update
  7.3 1.6 fusion.7
  13.9 0.7 compare_reduce_fusion.6
  14.6 0.7 compare_reduce_fusion.5
  15.9 0.6 compare_reduce_fusion.3
  16.5 0.7 compare_reduce_fusion.2
  17.2 0.7 compare_reduce_fusion.1
  17.9 0.6 compare_reduce_fusion
  18.5 100.8 %all-gather.4.cloned.1.call-done = f32[64,32768]{1,0:T(8,128)} async-done(((f32[64,1024]{1,0:T(8,128)}), f32[64,32768]{1,0:T(8,128)}) %all-gather.4.cloned.1.call-update) | async-done | bytes 8388624 | tf_op jit(solution)/shard_map/all_gather | solution.py:43
  119.3 1.5 select_select_fusion.5
  120.9 1.6 select_dynamic-update-slice_fusion
  122.4 1.5 fusion
  123.9 1.5 fusion.1
  125.5 1.5 fusion.2
  127.0 1.5 fusion.3
  128.6 1.5 fusion.4
  130.1 0.9 fusion.5
  131.0 0.7 copy-done.1
  131.8 42.2 %all-gather.6.cloned.1.call-done = f32[1024,1024]{1,0:T(8,128)} async-done(((f32[64,1024]{1,0:T(8,128)}), f32[1024,1024]{1,0:T(8,128)}) %all-gather.6.cloned.1.call-update) | async-done | bytes 4194320 | tf_op jit(solution)/shard_map/all_gather | solution.py:53
  174.0 13.0 %fusion.8 = f32[1024,768]{0,1:T(8,128)} fusion(f32[1024,1024]{1,0:T(8,128)} %all-gather.6.cloned.1.call-done, f32[1024,768]{1,0:T(8,128)S(1)} %copy-done), kind=kOutput, calls=%fused_computation.33 | convolution fusion | flops 9663676416 | bytes 10485760 | tf_op jit(solution)/shard_map/dot_general | solution.py:54
  187.1 45.9 %reduce-scatter.3.cloned.1.call-done = f32[1024,96]{0,1:T(8,128)} async-done(((f32[1024,768]{0,1:T(8,128)}), f32[1024,96]{0,1:T(8,128)}) %reduce-scatter.3.cloned.1.call-update) | async-done | bytes 393232 | tf_op jit(solution)/shard_map/reduce_scatter | solution.py:16
  233.0 28.4 %reduce-scatter.5.cloned.1.call-done = f32[1024,24]{0,1:T(8,128)} async-done(((f32[1024,96]{0,1:T(8,128)}), f32[1024,24]{0,1:T(8,128)}) %reduce-scatter.5.cloned.1.call-update) | async-done | bytes 98320 | tf_op jit(solution)/shard_map/reduce_scatter | solution.py:16
  261.5 0.9 sub.11
  262.4 10.4 %all_gather.14 = f32[1024,96]{0,1:T(8,128)} all-gather(f32[1024,24]{0,1:T(8,128)S(1)} %sub.11), channel_id=1, replica_groups=mesh['rows_0'=8,'rows_1'=4,'piv'=16] {'rows_1'}, dimensions={1}, use_global_device_ids=true | all-gather | bytes 491520 | tf_op jit(solution)/shard_map/all_gather | solution.py:22
  272.8 53.3 %all-gather.8.cloned.1.call-done = f32[1024,768]{0,1:T(8,128)} async-done(((f32[1024,96]{0,1:T(8,128)}), f32[1024,768]{0,1:T(8,128)}) %all-gather.8.cloned.1.call-update) | async-done | bytes 3145744 | tf_op jit(solution)/shard_map/all_gather | solution.py:22
  326.1 7.9 %fusion.9 = f32[1024,384]{1,0:T(8,128)} fusion(f32[1024,768]{0,1:T(8,128)} %all-gather.8.cloned.1.call-done, f32[768,384]{1,0:T(8,128)} %param.26), kind=kOutput, calls=%fused_computation.34 | convolution fusion | flops 3623878656 | bytes 5898240 | tf_op jit(solution)/shard_map/dot_general | solution.py:59
  334.0 7.6 %all-to-all-start = ((f32[16,64,384]{2,1,0:T(8,128)}), f32[16,64,384]{2,1,0:T(8,128)}, u32[]{:S(2)}, u32[]{:S(2)}) async-start(f32[16,64,384]{2,1,0:T(8,128)} %bitcast.31), calls=%async_computation.2 | async-start | bytes 3145728 | tf_op jit(solution)/shard_map/all_to_all | solution.py:34
  341.9 38.4 %all-to-all-done = f32[16,64,384]{2,1,0:T(8,128)} async-done(((f32[16,64,384]{2,1,0:T(8,128)}), f32[16,64,384]{2,1,0:T(8,128)}, u32[]{:S(2)}, u32[]{:S(2)}) %all-to-all-start) | async-done | bytes 1572896 | tf_op jit(solution)/shard_map/all_to_all | solution.py:34
  380.2 1.5 reduce_sum.9
  381.9 1.6 gather_fusion
  383.5 1.1 select_bitcast_fusion
  384.7 0.8 copy.10
  (27 shorter events, 1.2 us)
Async XLA Ops:
  6.5 167.4 %copy-start = (f32[1024,768]{1,0:T(8,128)S(1)}, f32[1024,768]{1,0:T(8,128)}, u32[]{:S(2)}) copy-start(f32[1024,768]{1,0:T(8,128)} %param.25) | copy-start | bytes 9437188
  6.5 112.8 %all-gather.4.cloned.1.call-start = ((), (), s32[]{:S(2)}) async-start(), calls=%async_computation.3 | async-start | bytes 8650752 | tf_op jit(solution)/shard_map/all_gather | solution.py:43
  7.3 166.7 %all-gather.6.cloned.1.call-start = ((), (), s32[]{:S(2)}) async-start(), calls=%async_computation.4 | async-start | bytes 4456448 | tf_op jit(solution)/shard_map/all_gather | solution.py:53
  131.0 0.7 copy-start.1
  131.7 101.2 %reduce-scatter.3.cloned.1.call-start = ((), (), s32[]{:S(2)}) async-start(), calls=%async_computation.5 | async-start | bytes 3538944 | tf_op jit(solution)/shard_map/reduce_scatter | solution.py:16
  187.0 74.5 %copy-start.2 = (f32[1024,24]{0,1:T(8,128)S(1)}, f32[1024,24]{0,1:T(8,128)}, u32[]{:S(2)}) copy-start(f32[1024,24]{0,1:T(8,128)} %param.27) | copy-start | bytes 294916
  187.0 74.4 %reduce-scatter.5.cloned.1.call-start = ((), (), s32[]{:S(2)}) async-start(), calls=%async_computation.6 | async-start | bytes 491520 | tf_op jit(solution)/shard_map/reduce_scatter | solution.py:16
  233.0 93.1 %all-gather.8.cloned.1.call-start = ((), (), s32[]{:S(2)}) async-start(), calls=%async_computation.7 | async-start | bytes 3538944 | tf_op jit(solution)/shard_map/all_gather | solution.py:22
  272.8 68.8 %copy-start.3 = (s32[4]{0:T(128)S(1)}, s32[4]{0:T(128)}, u32[]{:S(2)}) copy-start(s32[4]{0:T(128)} %param.28) | copy-start | bytes 52
  272.8 69.0 %copy-start.4 = (s32[4]{0:T(128)S(1)}, s32[4]{0:T(128)}, u32[]{:S(2)}) copy-start(s32[4]{0:T(128)} %param.29) | copy-start | bytes 52
  334.0 46.2 %all-to-all-start = ((f32[16,64,384]{2,1,0:T(8,128)}), f32[16,64,384]{2,1,0:T(8,128)}, u32[]{:S(2)}, u32[]{:S(2)}) async-start(f32[16,64,384]{2,1,0:T(8,128)} %bitcast.31), calls=%async_computation.2 | async-start | bytes 3145728 | tf_op jit(solution)/shard_map/all_to_all | solution.py:34
Sparse Core Ops, SparseCore 0:
  10.5 108.7 all-gather.3
  131.8 42.0 all-gather.5
  187.1 45.7 reduce-scatter.2
  235.6 25.7 reduce-scatter.4
  272.9 53.1 all-gather.7
where the time goes:
time: 393 us; the launch traced here: 392 us
  waiting for transfers between devices  310 us (79%)
  matrix products  21 us (5%)
  other arithmetic  20 us (5%)
  between operations  18.2 us (5%)
  blocking collectives  10.4 us (3%)
  starting transfers between devices  7.75 us (2%)
  local copies, waits for them, and re-layouts  4.88 us (1%)
    all_gather x1, waiting for transfers between devices, body(): piece = lax.all_gather(ancestor_sol, ROWS, axis=1, tiled=True)  101 us
    reduce_scatter x2, waiting for transfers between devices, scatter_axes(): nearer = lax.psum_scatter(value, axes[0], scatter_dimension=dim, tiled=True)  74.3 us
    all_gather x1, waiting for transfers between devices, gather_axes(): value = lax.all_gather(value, axis, axis=dim, tiled=True)  53.3 us
    all_gather x1, waiting for transfers between devices, body(): boundary = lax.all_gather(carry, 'piv', axis=0, tiled=True)  42.2 us
    all_to_all x1, waiting for transfers between devices, sent_and_summed(): lax.all_to_all(parts, axis, split_axis=0, concat_axis=0, tiled=True)  38.4 us
    dot_general x1, matrix products, body(): jnp.dot(boundary, lower_panel, precision=lax.Precision.HIGHEST, preferred...  13 us
    all_gather x1, blocking collectives, gather_axes(): value = lax.all_gather(value, axis, axis=dim, tiled=True)  10.4 us
    scatter x7, other arithmetic, body(): carry.at[:, block * ROW_BLK:(block + 1) * ROW_BLK]  10.1 us
  transfers between devices with their start and end apart: 6, of which 6 were waited for; matrix products, arithmetic and copies ran while one was open for 2% of the time, Pallas kernels for 0%

commit v1 on v0

--- a/solution.py
+++ b/solution.py
@@ -40,7 +40,9 @@
     count = front_map.shape[0]
     empty = jnp.zeros((local_srcs, count * ROW_BLK), jnp.float32)
     carry = empty
-    piece = lax.all_gather(ancestor_sol, ROWS, axis=1, tiled=True)
+    piece = jnp.concatenate(
+        lax.all_to_all(jnp.stack([ancestor_sol] * lax.axis_size(ROWS)), ROWS, 0, 0), axis=1
+    )
     width = piece.shape[1]
     for block in range(count):
         offset = front_map[block] * ROW_BLK

time: 393 us -> 495 us (1.26)
  waiting for transfers between devices: 310 us -> 396 us
  starting transfers between devices: 7.75 us -> 21.7 us
  local copies, waits for them, and re-layouts: 4.88 us -> 13.6 us
  other arithmetic: 20 us -> 13.5 us
    all_to_all x0 -> x1, waiting for transfers between devices: none -> 177 us  [body(): lax.all_to_all(jnp.stack([ancestor_sol] * lax.axis_size(ROWS)), ROWS, 0, 0)]
    all_gather x1 -> x0, waiting for transfers between devices: 101 us -> none  [body(): piece = lax.all_gather(ancestor_sol, ROWS, axis=1, tiled=True)]
    all_to_all x0 -> x1, starting transfers between devices: none -> 14 us  [body(): lax.all_to_all(jnp.stack([ancestor_sol] * lax.axis_size(ROWS)), ROWS, 0, 0)]
    all_gather x1, waiting for transfers between devices: 42.2 us -> 52.1 us  [body(): boundary = lax.all_gather(carry, 'piv', axis=0, tiled=True)]
    scatter x7, other arithmetic: 10.1 us -> 4.26 us  [body(): carry.at[:, block * ROW_BLK:(block + 1) * ROW_BLK]]
    another operation x0 -> x1, local copies, waits for them, and re-layouts: none -> 5.37 us  [body(): jnp.stack([ancestor_sol] * lax.axis_size(ROWS))]
  transfers between devices with their start and end apart: 6 -> 6, of which waited for: 6 -> 6; matrix products, arithmetic and copies ran while one was open for 2% -> 1% of each run, Pallas kernels for 0% -> 0%
where the time goes in v1:
time: 495 us; the launch traced here: 494 us
  waiting for transfers between devices  396 us (80%)
  starting transfers between devices  21.7 us (4%)
  matrix products  21 us (4%)
  between operations  18.4 us (4%)
  local copies, waits for them, and re-layouts  13.6 us (3%)
  other arithmetic  13.5 us (3%)
  blocking collectives  10.4 us (2%)
    all_to_all x1, waiting for transfers between devices, body(): lax.all_to_all(jnp.stack([ancestor_sol] * lax.axis_size(ROWS)), ROWS, 0, 0)  177 us
    reduce_scatter x2, waiting for transfers between devices, scatter_axes(): nearer = lax.psum_scatter(value, axes[0], scatter_dimension=dim, tiled=True)  74.5 us
    all_gather x1, waiting for transfers between devices, gather_axes(): value = lax.all_gather(value, axis, axis=dim, tiled=True)  53.4 us
    all_gather x1, waiting for transfers between devices, body(): boundary = lax.all_gather(carry, 'piv', axis=0, tiled=True)  52.1 us
    all_to_all x1, waiting for transfers between devices, sent_and_summed(): lax.all_to_all(parts, axis, split_axis=0, concat_axis=0, tiled=True)  38.4 us
    all_to_all x1, starting transfers between devices, body(): lax.all_to_all(jnp.stack([ancestor_sol] * lax.axis_size(ROWS)), ROWS, 0, 0)  14 us
    dot_general x1, matrix products, body(): jnp.dot(boundary, lower_panel, precision=lax.Precision.HIGHEST, preferred...  13 us
    all_gather x1, blocking collectives, gather_axes(): value = lax.all_gather(value, axis, axis=dim, tiled=True)  10.4 us
  transfers between devices with their start and end apart: 6, of which 6 were waited for; matrix products, arithmetic and copies ran while one was open for 1% of the time, Pallas kernels for 0%

profile of v1, /device:TPU:1, one launch (start us, length us, event | category | flops | bytes accessed | tf_op | source)
XLA Modules:
  0.0 494.1 jit_solution(4170344471010785743)
XLA Ops:
  6.5 5.4 %stack.2 = f32[32,64,1024]{2,1,0:T(8,128)} broadcast(f32[64,1024]{1,0:T(8,128)} %param.23), dimensions={1,2} | broadcast | bytes 8650752 | tf_op jit(solution)/shard_map/stack | solution.py:44
  11.9 14.0 %all-to-all-start = ((f32[32,64,1024]{2,1,0:T(8,128)}), f32[32,64,1024]{2,1,0:T(8,128)}, u32[]{:S(2)}, u32[]{:S(2)}) async-start(f32[32,64,1024]{2,1,0:T(8,128)} %stack.2), calls=%async_computation | async-start | bytes 16777216 | tf_op jit(solution)/shard_map/all_to_all | solution.py:44
  25.9 0.7 fusion.7
  31.8 0.7 compare_reduce_fusion.6
  32.5 0.6 compare_reduce_fusion.5
  33.7 0.7 compare_reduce_fusion.3
  34.4 0.7 compare_reduce_fusion.2
  35.1 0.7 compare_reduce_fusion.1
  35.8 0.7 compare_reduce_fusion
  36.4 177.1 %all-to-all-done = f32[32,64,1024]{2,1,0:T(8,128)} async-done(((f32[32,64,1024]{2,1,0:T(8,128)}), f32[32,64,1024]{2,1,0:T(8,128)}, u32[]{:S(2)}, u32[]{:S(2)}) %all-to-all-start) | async-done | bytes 8388640 | tf_op jit(solution)/shard_map/all_to_all | solution.py:44
  213.6 4.2 copy.14
  217.8 0.8 select_select_fusion.5
  218.6 0.6 select_dynamic-update-slice_fusion
  219.9 0.8 fusion.1
  220.6 0.7 fusion.2
  221.4 0.7 fusion.3
  222.1 0.7 fusion.4
  222.9 0.7 copy-done.1
  223.6 52.1 %all-gather.3.cloned.1.call-done = f32[1024,1024]{1,0:T(8,128)} async-done(((f32[64,1024]{1,0:T(8,128)}), f32[1024,1024]{1,0:T(8,128)}) %all-gather.3.cloned.1.call-update) | async-done | bytes 4194320 | tf_op jit(solution)/shard_map/all_gather | solution.py:55
  275.8 13.0 %fusion.8 = f32[1024,768]{0,1:T(8,128)} fusion(f32[1024,1024]{1,0:T(8,128)} %all-gather.3.cloned.1.call-done, f32[1024,768]{1,0:T(8,128)S(1)} %copy-done), kind=kOutput, calls=%fused_computation.33 | convolution fusion | flops 9663676416 | bytes 10485760 | tf_op jit(solution)/shard_map/dot_general | solution.py:56
  288.9 45.9 %reduce-scatter.3.cloned.1.call-done = f32[1024,96]{0,1:T(8,128)} async-done(((f32[1024,768]{0,1:T(8,128)}), f32[1024,96]{0,1:T(8,128)}) %reduce-scatter.3.cloned.1.call-update) | async-done | bytes 393232 | tf_op jit(solution)/shard_map/reduce_scatter | solution.py:16
  334.9 28.5 %reduce-scatter.5.cloned.1.call-done = f32[1024,24]{0,1:T(8,128)} async-done(((f32[1024,96]{0,1:T(8,128)}), f32[1024,24]{0,1:T(8,128)}) %reduce-scatter.5.cloned.1.call-update) | async-done | bytes 98320 | tf_op jit(solution)/shard_map/reduce_scatter | solution.py:16
  363.4 0.9 sub.11
  364.4 10.4 %all_gather.10 = f32[1024,96]{0,1:T(8,128)} all-gather(f32[1024,24]{0,1:T(8,128)S(1)} %sub.11), channel_id=1, replica_groups=mesh['rows_0'=8,'rows_1'=4,'piv'=16] {'rows_1'}, dimensions={1}, use_global_device_ids=true | all-gather | bytes 491520 | tf_op jit(solution)/shard_map/all_gather | solution.py:22
  374.8 53.4 %all-gather.5.cloned.1.call-done = f32[1024,768]{0,1:T(8,128)} async-done(((f32[1024,96]{0,1:T(8,128)}), f32[1024,768]{0,1:T(8,128)}) %all-gather.5.cloned.1.call-update) | async-done | bytes 3145744 | tf_op jit(solution)/shard_map/all_gather | solution.py:22
  428.2 7.9 %fusion.9 = f32[1024,384]{1,0:T(8,128)} fusion(f32[1024,768]{0,1:T(8,128)} %all-gather.5.cloned.1.call-done, f32[768,384]{1,0:T(8,128)} %param.26), kind=kOutput, calls=%fused_computation.34 | convolution fusion | flops 3623878656 | bytes 5898240 | tf_op jit(solution)/shard_map/dot_general | solution.py:61
  436.1 7.6 %all-to-all-start.1 = ((f32[16,64,384]{2,1,0:T(8,128)}), f32[16,64,384]{2,1,0:T(8,128)}, u32[]{:S(2)}, u32[]{:S(2)}) async-start(f32[16,64,384]{2,1,0:T(8,128)} %bitcast.42), calls=%async_computation.3 | async-start | bytes 3145728 | tf_op jit(solution)/shard_map/all_to_all | solution.py:34
  444.0 38.4 %all-to-all-done.1 = f32[16,64,384]{2,1,0:T(8,128)} async-done(((f32[16,64,384]{2,1,0:T(8,128)}), f32[16,64,384]{2,1,0:T(8,128)}, u32[]{:S(2)}, u32[]{:S(2)}) %all-to-all-start.1) | async-done | bytes 1572896 | tf_op jit(solution)/shard_map/all_to_all | solution.py:34
  482.4 1.5 reduce_sum.9
  484.0 1.6 gather_fusion
  485.6 1.1 select_bitcast_fusion
  486.8 0.8 copy.13
  (30 shorter events, 2.0 us)
Async XLA Ops:
  6.5 269.2 %copy-start = (f32[1024,768]{1,0:T(8,128)S(1)}, f32[1024,768]{1,0:T(8,128)}, u32[]{:S(2)}) copy-start(f32[1024,768]{1,0:T(8,128)} %param.25) | copy-start | bytes 9437188
  11.9 14.0 %copy-start.3 = (s32[8]{0:T(128)S(1)}, s32[8]{0:T(128)}, u32[]{:S(2)}) copy-start(s32[8]{0:T(128)} %param.24) | copy-start | bytes 100
  11.9 201.7 %all-to-all-start = ((f32[32,64,1024]{2,1,0:T(8,128)}), f32[32,64,1024]{2,1,0:T(8,128)}, u32[]{:S(2)}, u32[]{:S(2)}) async-start(f32[32,64,1024]{2,1,0:T(8,128)} %stack.2), calls=%async_computation | async-start | bytes 16777216 | tf_op jit(solution)/shard_map/all_to_all | solution.py:44
  25.9 249.9 %all-gather.3.cloned.1.call-start = ((), (), s32[]{:S(2)}) async-start(), calls=%async_computation.4 | async-start | bytes 4456448 | tf_op jit(solution)/shard_map/all_gather | solution.py:55
  222.9 0.7 copy-start.1
  223.6 111.2 %reduce-scatter.3.cloned.1.call-start = ((), (), s32[]{:S(2)}) async-start(), calls=%async_computation.5 | async-start | bytes 3538944 | tf_op jit(solution)/shard_map/reduce_scatter | solution.py:16
  288.8 74.6 %copy-start.2 = (f32[1024,24]{0,1:T(8,128)S(1)}, f32[1024,24]{0,1:T(8,128)}, u32[]{:S(2)}) copy-start(f32[1024,24]{0,1:T(8,128)} %param.27) | copy-start | bytes 294916
  288.8 74.6 %reduce-scatter.5.cloned.1.call-start = ((), (), s32[]{:S(2)}) async-start(), calls=%async_computation.6 | async-start | bytes 491520 | tf_op jit(solution)/shard_map/reduce_scatter | solution.py:16
  334.9 93.4 %all-gather.5.cloned.1.call-start = ((), (), s32[]{:S(2)}) async-start(), calls=%async_computation.7 | async-start | bytes 3538944 | tf_op jit(solution)/shard_map/all_gather | solution.py:22
  374.7 69.0 %copy-start.4 = (s32[4]{0:T(128)S(1)}, s32[4]{0:T(128)}, u32[]{:S(2)}) copy-start(s32[4]{0:T(128)} %param.28) | copy-start | bytes 52
  374.8 69.2 %copy-start.5 = (s32[4]{0:T(128)S(1)}, s32[4]{0:T(128)}, u32[]{:S(2)}) copy-start(s32[4]{0:T(128)} %param.29) | copy-start | bytes 52
  436.1 46.2 %all-to-all-start.1 = ((f32[16,64,384]{2,1,0:T(8,128)}), f32[16,64,384]{2,1,0:T(8,128)}, u32[]{:S(2)}, u32[]{:S(2)}) async-start(f32[16,64,384]{2,1,0:T(8,128)} %bitcast.42), calls=%async_computation.3 | async-start | bytes 3145728 | tf_op jit(solution)/shard_map/all_to_all | solution.py:34
Sparse Core Ops, SparseCore 0:
  223.7 52.0 all-gather.2
  289.0 45.8 reduce-scatter.2
  337.7 25.7 reduce-scatter.4
  374.9 53.2 all-gather.4
